TPU v7x, 32 devices: a whole 2x2x4 slice. The times are simulated.
32 devices in a mesh: store: 8 (over y, x, core), tp: 4 (over z).
Axes of the slice: x: 2, y: 2, z: 4, core: 2. Of those that a mesh axis runs over, the one named last changes fastest.
Arguments:
- hidden: bfloat16 [8, 576, 8192], P('store', None, 'tp'), may hold values from -300 to 300
- w_query: bfloat16 [8192, 4096], P(None, 'tp'), may hold values from -0.0625 to 0.0625
- w_keyvalue: bfloat16 [8192, 1024], P('tp'), may hold values from -0.1875 to 0.1875
- passage_cache: bfloat16 [32, 4, 384, 256], P('store'), may hold values from -400 to 400
- passage_ids: int32 [8, 8], replicated, may hold values from 0 to 31, as said below
- select_index: int32 [8, 576], P('store'), may hold values from 0 to 3071, as said below
- select_count: int32 [8], P('store'), may hold values from 288 to 576, as said below
Outputs:
- context: bfloat16 [8, 576, 4096], P('store', None, 'tp')
Inputs may be any that keep to these rules, and one draw needn't show every extreme that they name: `passage_ids`: the passages of one prompt lie in distinct shards of the pool, shard = id // 4. `select_index`: all entries of a row are distinct positions of the prompt; the first select_count[p] of row p are in increasing order, the others are ignored. `select_count`: some prompt of every draw has 576 selected tokens.
All inputs are finite; a program needn't handle non-finite values.
Results may differ from a plain program's by a relative error of at most 0.04.
Values may be sent and summed in bfloat16 or wider, within the bound.
No kernel may reach another device: no remote copies, remote signals or barrier semaphores. Data moves between devices by JAX's collectives and lax.ppermute only.
A program may use at most 128 MiB of HBM per device.

v0:
```python
import jax
import jax.numpy as jnp
from jax import lax
from jax.sharding import PartitionSpec as P

D = 8192
KV_HEADS = 4
HEAD_DIM = 128
PASSAGE = 384
PASSAGES = 8
SEQ = 3072
ROPE_BASE = 1000000.0
EPSILON = 1e-06


def rotate(vectors, positions):
    half_dim = vectors.shape[-1] // 2
    frequency = ROPE_BASE ** (-(jnp.arange(half_dim, dtype=jnp.float32) * 2.0) / vectors.shape[-1])
    angles = positions.astype(jnp.float32)[..., None] * frequency
    cosine = jnp.cos(angles)
    sine_part = jnp.sin(angles)
    front_half = vectors[..., :half_dim]
    back_half = vectors[..., half_dim:]
    return jnp.concatenate(
        [front_half * cosine - back_half * sine_part, back_half * cosine + front_half * sine_part],
        axis=-1,
    )


def local(hidden, w_query, w_keyvalue, passage_cache, passage_ids, select_index, select_count):
    tp_count = lax.axis_size("tp")
    group_width = tp_count // KV_HEADS
    tp_rank = lax.axis_index("tp")
    kv_head = tp_rank // group_width
    store_rank = lax.axis_index("store")
    local_heads = w_query.shape[1] // HEAD_DIM
    row_count = hidden.shape[1]
    pool_dev = passage_cache.shape[0]
    partial_kv = jnp.dot(hidden[0], w_keyvalue, preferred_element_type=jnp.float32)
    proj_kv = lax.psum(partial_kv, "tp")
    head_kv = lax.dynamic_slice_in_dim(proj_kv, kv_head * 2 * HEAD_DIM, 2 * HEAD_DIM, 1)
    token_part = lax.all_gather(hidden, "tp", axis=2, tiled=True)[0]
    widened = token_part.astype(jnp.float32)
    running = jnp.dot(token_part, w_query, preferred_element_type=jnp.float32)
    squares = jnp.sum(widened * widened, axis=-1)
    inverse_rms = lax.rsqrt(squares / D + EPSILON)
    positions = select_index[0]
    live_count = select_count[0]
    queries = rotate(
        (running * inverse_rms[:, None]).reshape(row_count, local_heads, HEAD_DIM),
        positions[:, None],
    )
    queries = (queries * HEAD_DIM ** (-0.5)).astype(jnp.bfloat16)
    key_value = head_kv * inverse_rms[:, None]
    new_keys = rotate(key_value[:, :HEAD_DIM], positions).astype(jnp.bfloat16)
    new_values = key_value[:, HEAD_DIM:].astype(jnp.bfloat16)
    head_cache = lax.dynamic_index_in_dim(passage_cache, kv_head, 1, keepdims=False)
    owners = passage_ids // pool_dev
    local_index = passage_ids % pool_dev
    matches = owners == store_rank
    local_slot = jnp.sum(jnp.where(matches, local_index, 0), axis=1)
    present = jnp.any(matches, axis=1)
    outgoing = jnp.take(head_cache, local_slot, axis=0) * present[:, None, None].astype(
        jnp.bfloat16
    )
    incoming = lax.all_to_all(outgoing, "store", split_axis=0, concat_axis=0, tiled=True)
    my_owners = lax.dynamic_index_in_dim(owners, store_rank, 0, keepdims=False)
    fetched = jnp.take(incoming, my_owners, axis=0)
    offsets = jnp.arange(PASSAGES) * PASSAGE
    old_keys = rotate(fetched[..., :HEAD_DIM].astype(jnp.float32), offsets[:, None]).astype(
        jnp.bfloat16
    )
    old_keys = old_keys.reshape(SEQ, HEAD_DIM)
    old_values = fetched[..., HEAD_DIM:].reshape(SEQ, HEAD_DIM)
    row_ids = jnp.arange(row_count, dtype=jnp.int32)
    target = jnp.where(row_ids < live_count, positions, SEQ)
    all_keys = old_keys.at[target].set(new_keys, mode="drop")
    all_values = old_values.at[target].set(new_values, mode="drop")
    allowed = jnp.arange(SEQ, dtype=jnp.int32)[None, :] <= positions[:, None]
    scores = jnp.einsum("rgd,sd->grs", queries, all_keys, preferred_element_type=jnp.float32)
    scores = jnp.where(allowed[None], scores, -jnp.inf)
    row_max = jnp.max(scores, axis=-1, keepdims=True)
    shifted = jnp.exp(scores - row_max)
    weight = (shifted / jnp.sum(shifted, axis=-1, keepdims=True)).astype(jnp.bfloat16)
    context = jnp.einsum("grs,sd->rgd", weight, all_values, preferred_element_type=jnp.float32)
    row_live = (row_ids < live_count)[:, None, None]
    context = jnp.where(row_live, context, 0.0)
    return context.reshape(1, row_count, local_heads * HEAD_DIM).astype(jnp.bfloat16)


def solution(mesh):
    in_specs = (
        P("store", None, "tp"),
        P(None, "tp"),
        P("tp", None),
        P("store", None, None, None),
        P(),
        P("store", None),
        P("store"),
    )
    out_specs = P("store", None, "tp")
    return jax.shard_map(local, mesh=mesh, in_specs=in_specs, out_specs=out_specs, check_vma=False)
```

profile of v0, /device:TPU:0, one launch (start us, length us, event | category | flops | bytes accessed | tf_op | source)
XLA Modules:
  0.0 357.8 jit_solution(9565624965004974671)
XLA Ops:
  6.5 0.0 copy-start
  6.5 0.0 copy-start.5
  6.5 0.0 all-gather.2.cloned.1.call-start
  6.5 0.7 all-gather.2.cloned.1.call-update
  7.3 0.1 copy-done.5
  7.4 0.1 fusion.36
  7.5 0.1 fusion.29
  7.6 0.8 copy-done
  8.4 0.9 dynamic-slice_bitcast_fusion
  9.4 1.8 gather_fusion
  11.2 1.3 select_multiply_fusion
  12.5 5.2 %all-to-all-start = ((bf16[8,384,256]{2,1,0:T(8,128)(2,1)}), bf16[8,384,256]{2,1,0:T(8,128)(2,1)S(1)}, u32[]{:S(2)}, u32[]{:S(2)}) async-start(bf16[8,384,256]{2,1,0:T(8,128)(2,1)} %select_multiply_fusion), calls=%async_computation | async-start | bytes 3145728 | tf_op jit(solution)/shard_map/all_to_all | solution.py:66
  17.7 0.0 all-reduce.2.cloned.1.call-start
  17.8 7.9 %fusion.10 = f32[576,1024]{1,0:T(8,128)} fusion(bf16[2048,1024]{1,0:T(8,128)(2,1)} %param.9, bf16[1,576,2048]{2,1,0:T(8,128)(2,1)} %param.7), kind=kOutput, calls=%fused_computation.19 | convolution fusion | flops 2415919104 | bytes 8912896 | tf_op jit(solution)/shard_map/dot_general | solution.py:39
  25.7 0.0 copy-start.6
  25.7 0.0 all-reduce.2.cloned.1.call-update
  26.4 0.0 copy-done.6
  26.5 0.1 multiply_cosine_fusion.1
  26.7 2.6 iota_compare_fusion
  29.2 9.5 %all-to-all-done = bf16[8,384,256]{2,1,0:T(8,128)(2,1)S(1)} async-done(((bf16[8,384,256]{2,1,0:T(8,128)(2,1)}), bf16[8,384,256]{2,1,0:T(8,128)(2,1)S(1)}, u32[]{:S(2)}, u32[]{:S(2)}) %all-to-all-start) | async-done | bytes 1572896 | tf_op jit(solution)/shard_map/all_to_all | solution.py:66
  38.7 1.8 gather_fusion.1
  40.5 1.6 broadcast_select_fusion
  42.1 1.1 fusion.38
  43.3 0.6 subtract_convert_fusion
  43.9 1.3 pad_maximum_fusion
  45.2 133.2 %all-gather.2.cloned.1.call-done = bf16[1,576,8192]{2,1,0:T(8,128)(2,1)} async-done(((bf16[1,576,2048]{2,1,0:T(8,128)(2,1)}), bf16[1,576,8192]{2,1,0:T(8,128)(2,1)}) %all-gather.2.cloned.1.call-update) | async-done | bytes 9437200 | tf_op jit(solution)/shard_map/all_gather | solution.py:42
  178.4 0.0 copy-start.2
  178.4 5.8 %multiply_reduce_fusion = f32[576]{0:T(1024)S(1)} fusion(bf16[1,576,8192]{2,1,0:T(8,128)(2,1)} %all-gather.2.cloned.1.call-done), kind=kLoop, calls=%fused_computation.12 | loop fusion | flops 14155200 | bytes 9439488 | tf_op jit(solution)/shard_map/reduce_sum | solution.py:45
  184.2 0.9 copy-done.2
  185.1 13.6 %multiply_bitcast_fusion = f32[72,8,8,128]{3,1,2,0:T(8,128)S(1)} fusion(bf16[8192,1024]{1,0:T(8,128)(2,1)} %param.8, bf16[1,576,8192]{2,1,0:T(8,128)(2,1)S(1)} %copy-done.2, f32[576]{0:T(1024)S(1)} %add_rsqrt_fusion), kind=kOutput, calls=%fused_computation.24 | convolution fusion | flops 9664266240 | bytes 28576000 | tf_op jit(solution)/shard_map/dot_general | solution.py:44
  198.7 0.5 copy.15
  199.2 2.9 fusion.37
  202.1 0.0 copy-start.3
  202.1 71.5 %all-reduce.2.cloned.1.call-done = f32[576,1024]{1,0:T(8,128)} async-done(((f32[576,1024]{1,0:T(8,128)}), f32[576,1024]{1,0:T(8,128)}) %all-reduce.2.cloned.1.call-update) | async-done | bytes 2359312 | tf_op jit(solution)/shard_map/psum | solution.py:40
  273.6 1.2 dynamic-slice_multiply_fusion
  274.9 2.1 subtract_convert_fusion.1
  276.9 6.4 %scatter_custom_fusion = bf16[3072,128]{1,0:T(8,128)(2,1)} fusion(bf16[3072,128]{1,0:T(8,128)(2,1)} %bitcast.68, s32[576]{0:T(1024)S(1)} %fusion.32, f32[576,256]{1,0:T(8,128)S(1)} %dynamic-slice_multiply_fusion), kind=kCustom, calls=%fused_computation.43 | custom fusion | bytes 933888 | tf_op jit(solution)/shard_map/scatter | solution.py:78
  283.3 7.2 %scatter_custom_fusion.1 = bf16[3072,128]{1,0:T(8,128)(2,1)} fusion(bf16[3072,128]{1,0:T(8,128)(2,1)} %pad_maximum_fusion, s32[576]{0:T(1024)S(1)} %fusion.32, bf16[576,64]{1,0:T(8,128)(2,1)} %get-tuple-element.17, bf16[]{:T(256)} %constant.123, bf16[576,64]{1,0:T(8,128)(2,1)S(1)} %get-tuple-element.16), kind=kCustom, calls=%fused_computation.44 | custom fusion | flops 294912 | bytes 1081856 | tf_op jit(solution)/shard_map/scatter | solution.py:77
  290.5 0.0 copy-done.3
  290.5 0.0 copy-start.4
  290.5 4.7 %multiply_subtract_fusion = (f32[576,8,64]{2,0,1:T(8,128)}, f32[576,8,64]{2,0,1:T(8,128)}) fusion(f32[576,8,64]{2,1,0:T(8,128)} %get-tuple-element.11, f32[576,8,64]{2,1,0:T(8,128)S(1)} %copy-done.3, f32[576,64]{1,0:T(8,128)S(1)} %get-tuple-element.18, f32[576,64]{1,0:T(8,128)} %get-tuple-element.19), kind=kLoop, calls=%fused_computation.23 | loop fusion | flops 1769472 | bytes 5013504 | tf_op jit(solution)/shard_map/sub | solution.py:25
  295.2 0.0 copy-done.4
  295.2 28.2 %fusion.39 = (f32[8,576]{1,0:T(8,128)S(1)}, f32[8,576,3072]{2,1,0:T(8,128)}) fusion(pred[576,3072]{1,0:T(8,128)(4,1)} %iota_compare_fusion, bf16[3072,128]{1,0:T(8,128)(2,1)S(1)} %copy-done.4, f32[576,8,64]{2,0,1:T(8,128)} %get-tuple-element.9, f32[576,8,64]{2,0,1:T(8,128)} %get-tuple-element.8), kind=kOutput, calls=%fused_computation.83 | convolution fusion | flops 3668118528 | bytes 61556736 | tf_op jit(solution)/shard_map/sub | solution.py:83
  323.4 0.0 copy-start.1
  323.4 21.4 %fusion.14 = bf16[576,8,128]{2,0,1:T(8,128)(2,1)} fusion(f32[8,576,3072]{2,1,0:T(8,128)} %get-tuple-element.23, f32[8,576]{1,0:T(8,128)S(1)} %get-tuple-element.22, pred[576]{0:T(1024)(128)(4,1)S(1)} %iota_compare_fusion.1, bf16[3072,128]{1,0:T(8,128)(2,1)} %scatter_custom_fusion), kind=kOutput, calls=%fused_computation.29 | convolution fusion | flops 3653369856 | bytes 58608192 | tf_op jit(solution)/shard_map/grs,sd->rgd/dot_general | solution.py:85
  344.9 3.0 copy.12
  347.9 3.0 convert_element_type.79
  351.0 0.0 copy-done.1
  (14 shorter events, 0.1 us)
Async XLA Ops:
  6.5 1.9 copy-start
  6.5 0.8 copy-start.5
  6.5 171.9 %all-gather.2.cloned.1.call-start = ((), (), s32[]{:S(2)}) async-start(), calls=%async_computation.2 | async-start | bytes 11796480 | tf_op jit(solution)/shard_map/all_gather | solution.py:42
  12.5 26.2 %all-to-all-start = ((bf16[8,384,256]{2,1,0:T(8,128)(2,1)}), bf16[8,384,256]{2,1,0:T(8,128)(2,1)S(1)}, u32[]{:S(2)}, u32[]{:S(2)}) async-start(bf16[8,384,256]{2,1,0:T(8,128)(2,1)} %select_multiply_fusion), calls=%async_computation | async-start | bytes 3145728 | tf_op jit(solution)/shard_map/all_to_all | solution.py:66
  17.7 255.9 %all-reduce.2.cloned.1.call-start = ((), (), s32[]{:S(2)}) async-start(), calls=%async_computation.1 | async-start | bytes 4718592 | tf_op jit(solution)/shard_map/psum | solution.py:40
  25.7 0.7 copy-start.6
  178.4 6.6 %copy-start.2 = (bf16[1,576,8192]{2,1,0:T(8,128)(2,1)S(1)}, bf16[1,576,8192]{2,1,0:T(8,128)(2,1)}, u32[]{:S(2)}) copy-start(bf16[1,576,8192]{2,1,0:T(8,128)(2,1)} %all-gather.2.cloned.1.call-done) | copy-start | bytes 28311556
  202.1 88.4 %copy-start.3 = (f32[576,8,64]{2,1,0:T(8,128)S(1)}, f32[576,8,64]{2,1,0:T(8,128)}, u32[]{:S(2)}) copy-start(f32[576,8,64]{2,1,0:T(8,128)} %get-tuple-element.10) | copy-start | bytes 3538948
  290.5 4.7 %copy-start.4 = (bf16[3072,128]{1,0:T(8,128)(2,1)S(1)}, bf16[3072,128]{1,0:T(8,128)(2,1)}, u32[]{:S(2)}) copy-start(bf16[3072,128]{1,0:T(8,128)(2,1)} %scatter_custom_fusion.1) | copy-start | bytes 2359300
  323.4 27.5 %copy-start.1 = (bf16[4,4,384,256]{3,2,1,0:T(8,128)(2,1)S(1)}, bf16[4,4,384,256]{3,2,1,0:T(8,128)(2,1)}, u32[]{:S(2)}) copy-start(bf16[4,4,384,256]{3,2,1,0:T(8,128)(2,1)} %param.10) | copy-start | bytes 9437188
Sparse Core Ops, SparseCore 0:
  8.9 169.4 all-gather.1
  180.8 92.8 all-reduce.1
where the time goes:
time: 358 us
  waiting for transfers between devices  215 us (60%)
  matrix products  71.2 us (20%)
  other arithmetic  30 us (8%)
  local copies, waits for them, and re-layouts  22.3 us (6%)
  between operations  14.2 us (4%)
  starting transfers between devices  5.24 us (1%)
    all_gather x1, waiting for transfers between devices, local(): token_part = lax.all_gather(hidden, 'tp', axis=2, tiled=True)[0]  133 us
    psum x1, waiting for transfers between devices, local(): proj_kv = lax.psum(partial_kv, 'tp')  71.5 us
    sub x1, matrix products, local(): shifted = jnp.exp(scores - row_max)  28.2 us
    dot_general x1, matrix products, local(): jnp.einsum('grs,sd->rgd', weight, all_values, preferred_element_type=jnp....  21.4 us
    dot_general x1, matrix products, local(): running = jnp.dot(token_part, w_query, preferred_element_type=jnp.float32)  13.6 us
    all_to_all x1, waiting for transfers between devices, local(): lax.all_to_all(outgoing, 'store', split_axis=0, concat_axis=0, tiled=True)  9.47 us
    dot_general x1, matrix products, local(): jnp.dot(hidden[0], w_keyvalue, preferred_element_type=jnp.float32)  7.94 us
  transfers between devices with their start and end apart: 3, of which 3 were waited for; matrix products, arithmetic and copies ran while one was open for 12% of the time, Pallas kernels for 0%

commit v1 on v0

--- a/solution.py
+++ b/solution.py
@@ -37,7 +37,8 @@
     row_count = hidden.shape[1]
     pool_dev = passage_cache.shape[0]
     partial_kv = jnp.dot(hidden[0], w_keyvalue, preferred_element_type=jnp.float32)
-    proj_kv = lax.psum(partial_kv, "tp")
+    supply_outputs = lambda shard_in: lax.all_gather(shard_in, axis_name="tp").sum(axis=0)
+    proj_kv = supply_outputs(partial_kv)
     head_kv = lax.dynamic_slice_in_dim(proj_kv, kv_head * 2 * HEAD_DIM, 2 * HEAD_DIM, 1)
     token_part = lax.all_gather(hidden, "tp", axis=2, tiled=True)[0]
     widened = token_part.astype(jnp.float32)

time: 358 us -> 436 us (1.22)
  waiting for transfers between devices: 215 us -> 286 us
  other arithmetic: 30 us -> 36.7 us
    all_gather x0 -> x1, waiting for transfers between devices: none -> 142 us  [local(): lax.all_gather(shard_in, axis_name='tp').sum(axis=0)]
    psum x1 -> x0, waiting for transfers between devices: 71.5 us -> none  [local(): proj_kv = lax.psum(partial_kv, 'tp')]
    all_to_all x1, waiting for transfers between devices: 9.47 us -> 17.5 us  [local(): lax.all_to_all(outgoing, 'store', split_axis=0, concat_axis=0, tiled=True)]
    all_gather x1, waiting for transfers between devices: 133 us -> 126 us  [local(): token_part = lax.all_gather(hidden, 'tp', axis=2, tiled=True)[0]]
    reduce_sum x0 -> x1, other arithmetic: none -> 6.44 us  [local(): lax.all_gather(shard_in, axis_name='tp').sum(axis=0)]
  transfers between devices with their start and end apart: 3 -> 3, of which waited for: 3 -> 3; matrix products, arithmetic and copies ran while one was open for 12% -> 10% of each run, Pallas kernels for 0% -> 0%
where the time goes in v1:
time: 436 us
  waiting for transfers between devices  286 us (66%)
  matrix products  70.7 us (16%)
  other arithmetic  36.7 us (8%)
  local copies, waits for them, and re-layouts  22.2 us (5%)
  between operations  14.2 us (3%)
  starting transfers between devices  5.48 us (1%)
    all_gather x1, waiting for transfers between devices, local(): lax.all_gather(shard_in, axis_name='tp').sum(axis=0)  142 us
    all_gather x1, waiting for transfers between devices, local(): token_part = lax.all_gather(hidden, 'tp', axis=2, tiled=True)[0]  126 us
    sub x1, matrix products, local(): shifted = jnp.exp(scores - row_max)  28 us
    dot_general x1, matrix products, local(): jnp.einsum('grs,sd->rgd', weight, all_values, preferred_element_type=jnp....  21.4 us
    all_to_all x1, waiting for transfers between devices, local(): lax.all_to_all(outgoing, 'store', split_axis=0, concat_axis=0, tiled=True)  17.5 us
    dot_general x1, matrix products, local(): running = jnp.dot(token_part, w_query, preferred_element_type=jnp.float32)  14.2 us
  transfers between devices with their start and end apart: 3, of which 3 were waited for; matrix products, arithmetic and copies ran while one was open for 10% of the time, Pallas kernels for 0%

profile of v1, /device:TPU:0, one launch (start us, length us, event | category | flops | bytes accessed | tf_op | source)
XLA Modules:
  0.0 435.7 jit_solution(4381174869794242931)
XLA Ops:
  6.5 0.0 copy-start
  6.5 0.0 all-gather.4.cloned.1.call-start
  6.5 0.7 all-gather.4.cloned.1.call-update
  7.3 0.0 all-gather.6.cloned.1.call-start
  7.3 7.1 %fusion.10 = f32[576,1024]{1,0:T(8,128)} fusion(bf16[2048,1024]{1,0:T(8,128)(2,1)} %param.9, bf16[1,576,2048]{2,1,0:T(8,128)(2,1)} %param.7), kind=kOutput, calls=%fused_computation.19 | convolution fusion | flops 2415919104 | bytes 8912896 | tf_op jit(solution)/shard_map/dot_general | solution.py:39
  14.4 0.0 copy-start.5
  14.4 0.0 all-gather.6.cloned.1.call-update
  14.4 0.7 copy-done.5
  15.1 0.1 fusion.36
  15.2 0.1 fusion.29
  15.3 0.0 copy-done
  15.3 0.9 dynamic-slice_bitcast_fusion
  16.3 1.8 gather_fusion
  18.1 1.4 select_multiply_fusion
  19.5 0.0 copy-start.6
  19.5 5.4 %all-to-all-start = ((bf16[8,384,256]{2,1,0:T(8,128)(2,1)}), bf16[8,384,256]{2,1,0:T(8,128)(2,1)S(1)}, u32[]{:S(2)}, u32[]{:S(2)}) async-start(bf16[8,384,256]{2,1,0:T(8,128)(2,1)} %select_multiply_fusion), calls=%async_computation | async-start | bytes 3145728 | tf_op jit(solution)/shard_map/all_to_all | solution.py:67
  25.6 0.0 copy-done.6
  25.7 0.1 multiply_cosine_fusion.1
  25.8 2.6 iota_compare_fusion
  28.4 17.5 %all-to-all-done = bf16[8,384,256]{2,1,0:T(8,128)(2,1)S(1)} async-done(((bf16[8,384,256]{2,1,0:T(8,128)(2,1)}), bf16[8,384,256]{2,1,0:T(8,128)(2,1)S(1)}, u32[]{:S(2)}, u32[]{:S(2)}) %all-to-all-start) | async-done | bytes 1572896 | tf_op jit(solution)/shard_map/all_to_all | solution.py:67
  45.9 1.8 gather_fusion.1
  47.8 1.6 broadcast_select_fusion
  49.4 1.1 fusion.38
  50.5 0.6 subtract_convert_fusion
  51.1 1.3 pad_maximum_fusion
  52.5 126.0 %all-gather.4.cloned.1.call-done = bf16[1,576,8192]{2,1,0:T(8,128)(2,1)} async-done(((bf16[1,576,2048]{2,1,0:T(8,128)(2,1)}), bf16[1,576,8192]{2,1,0:T(8,128)(2,1)}) %all-gather.4.cloned.1.call-update) | async-done | bytes 9437200 | tf_op jit(solution)/shard_map/all_gather | solution.py:43
  178.4 0.0 copy-start.2
  178.4 5.8 %multiply_reduce_fusion = f32[576]{0:T(1024)S(1)} fusion(bf16[1,576,8192]{2,1,0:T(8,128)(2,1)} %all-gather.4.cloned.1.call-done), kind=kLoop, calls=%fused_computation.12 | loop fusion | flops 14155200 | bytes 9439488 | tf_op jit(solution)/shard_map/reduce_sum | solution.py:46
  184.2 0.7 copy-done.2
  184.9 14.2 %multiply_bitcast_fusion = f32[72,8,8,128]{3,1,2,0:T(8,128)S(1)} fusion(bf16[8192,1024]{1,0:T(8,128)(2,1)} %param.8, bf16[1,576,8192]{2,1,0:T(8,128)(2,1)S(1)} %copy-done.2, f32[576]{0:T(1024)S(1)} %add_rsqrt_fusion), kind=kOutput, calls=%fused_computation.24 | convolution fusion | flops 9664266240 | bytes 28576000 | tf_op jit(solution)/shard_map/dot_general | solution.py:45
  199.1 0.5 copy.15
  199.6 3.0 fusion.37
  202.6 142.3 %all-gather.6.cloned.1.call-done = f32[2304,1024]{1,0:T(8,128)} async-done(((f32[576,1024]{1,0:T(8,128)}), f32[2304,1024]{1,0:T(8,128)}) %all-gather.6.cloned.1.call-update) | async-done | bytes 9437200 | tf_op jit(solution)/shard_map/all_gather | solution.py:40
  345.0 6.4 %reduce_sum.40 = f32[576,1024]{1,0:T(8,128)} reduce(f32[4,576,1024]{2,1,0:T(8,128)} %bitcast.67, f32[]{:T(128)} %constant.105.clone.1), dimensions={0}, to_apply=%region_2.3 | reduce | flops 1769472 | bytes 11796484 | tf_op jit(solution)/shard_map/reduce_sum | solution.py:40
  351.4 0.0 copy-start.3
  351.4 1.4 dynamic-slice_multiply_fusion
  352.8 2.1 subtract_convert_fusion.1
  354.8 6.7 %scatter_custom_fusion = bf16[3072,128]{1,0:T(8,128)(2,1)} fusion(bf16[3072,128]{1,0:T(8,128)(2,1)} %bitcast.70, s32[576]{0:T(1024)S(1)} %fusion.32, f32[576,256]{1,0:T(8,128)S(1)} %dynamic-slice_multiply_fusion), kind=kCustom, calls=%fused_computation.43 | custom fusion | bytes 933888 | tf_op jit(solution)/shard_map/scatter | solution.py:79
  361.5 7.2 %scatter_custom_fusion.1 = bf16[3072,128]{1,0:T(8,128)(2,1)} fusion(bf16[3072,128]{1,0:T(8,128)(2,1)} %pad_maximum_fusion, s32[576]{0:T(1024)S(1)} %fusion.32, bf16[576,64]{1,0:T(8,128)(2,1)} %get-tuple-element.17, bf16[]{:T(256)} %constant.123, bf16[576,64]{1,0:T(8,128)(2,1)S(1)} %get-tuple-element.16), kind=kCustom, calls=%fused_computation.44 | custom fusion | flops 294912 | bytes 1081856 | tf_op jit(solution)/shard_map/scatter | solution.py:78
  368.6 0.0 copy-done.3
  368.6 0.0 copy-start.4
  368.6 4.7 %multiply_subtract_fusion = (f32[576,8,64]{2,0,1:T(8,128)}, f32[576,8,64]{2,0,1:T(8,128)}) fusion(f32[576,8,64]{2,1,0:T(8,128)} %get-tuple-element.11, f32[576,8,64]{2,1,0:T(8,128)S(1)} %copy-done.3, f32[576,64]{1,0:T(8,128)S(1)} %get-tuple-element.18, f32[576,64]{1,0:T(8,128)} %get-tuple-element.19), kind=kLoop, calls=%fused_computation.23 | loop fusion | flops 1769472 | bytes 5013504 | tf_op jit(solution)/shard_map/sub | solution.py:25
  373.4 0.0 copy-done.4
  373.4 28.0 %fusion.39 = (f32[8,576]{1,0:T(8,128)S(1)}, f32[8,576,3072]{2,1,0:T(8,128)}) fusion(pred[576,3072]{1,0:T(8,128)(4,1)} %iota_compare_fusion, bf16[3072,128]{1,0:T(8,128)(2,1)S(1)} %copy-done.4, f32[576,8,64]{2,0,1:T(8,128)} %get-tuple-element.9, f32[576,8,64]{2,0,1:T(8,128)} %get-tuple-element.8), kind=kOutput, calls=%fused_computation.83 | convolution fusion | flops 3668118528 | bytes 61556736 | tf_op jit(solution)/shard_map/sub | solution.py:84
  401.4 21.4 %fusion.14 = bf16[576,8,128]{2,0,1:T(8,128)(2,1)} fusion(f32[8,576,3072]{2,1,0:T(8,128)} %get-tuple-element.23, f32[8,576]{1,0:T(8,128)S(1)} %get-tuple-element.22, pred[576]{0:T(1024)(128)(4,1)S(1)} %iota_compare_fusion.1, bf16[3072,128]{1,0:T(8,128)(2,1)} %scatter_custom_fusion), kind=kOutput, calls=%fused_computation.29 | convolution fusion | flops 3653369856 | bytes 58608192 | tf_op jit(solution)/shard_map/grs,sd->rgd/dot_general | solution.py:86
  422.8 3.0 copy.12
  425.8 3.0 convert_element_type.79
  428.9 0.0 copy-done.1
  (15 shorter events, 0.1 us)
Async XLA Ops:
  6.5 8.8 %copy-start = (bf16[4,4,384,256]{3,2,1,0:T(8,128)(2,1)S(1)}, bf16[4,4,384,256]{3,2,1,0:T(8,128)(2,1)}, u32[]{:S(2)}) copy-start(bf16[4,4,384,256]{3,2,1,0:T(8,128)(2,1)} %param.10) | copy-start | bytes 9437188
  6.5 171.9 %all-gather.4.cloned.1.call-start = ((), (), s32[]{:S(2)}) async-start(), calls=%async_computation.1 | async-start | bytes 11796480 | tf_op jit(solution)/shard_map/all_gather | solution.py:43
  7.3 337.7 %all-gather.6.cloned.1.call-start = ((), (), s32[]{:S(2)}) async-start(), calls=%async_computation.2 | async-start | bytes 11796480 | tf_op jit(solution)/shard_map/all_gather | solution.py:40
  14.4 0.7 copy-start.5
  19.5 6.1 %copy-start.6 = (s32[1,576]{1,0:T(1,128)S(1)}, s32[1,576]{1,0:T(1,128)}, u32[]{:S(2)}) copy-start(s32[1,576]{1,0:T(1,128)} %param.12) | copy-start | bytes 6916
  19.5 26.4 %all-to-all-start = ((bf16[8,384,256]{2,1,0:T(8,128)(2,1)}), bf16[8,384,256]{2,1,0:T(8,128)(2,1)S(1)}, u32[]{:S(2)}, u32[]{:S(2)}) async-start(bf16[8,384,256]{2,1,0:T(8,128)(2,1)} %select_multiply_fusion), calls=%async_computation | async-start | bytes 3145728 | tf_op jit(solution)/shard_map/all_to_all | solution.py:67
  178.4 6.5 %copy-start.2 = (bf16[1,576,8192]{2,1,0:T(8,128)(2,1)S(1)}, bf16[1,576,8192]{2,1,0:T(8,128)(2,1)}, u32[]{:S(2)}) copy-start(bf16[1,576,8192]{2,1,0:T(8,128)(2,1)} %all-gather.4.cloned.1.call-done) | copy-start | bytes 28311556
  351.4 17.2 %copy-start.3 = (f32[576,8,64]{2,1,0:T(8,128)S(1)}, f32[576,8,64]{2,1,0:T(8,128)}, u32[]{:S(2)}) copy-start(f32[576,8,64]{2,1,0:T(8,128)} %get-tuple-element.10) | copy-start | bytes 3538948
  368.6 4.7 %copy-start.4 = (bf16[3072,128]{1,0:T(8,128)(2,1)S(1)}, bf16[3072,128]{1,0:T(8,128)(2,1)}, u32[]{:S(2)}) copy-start(bf16[3072,128]{1,0:T(8,128)(2,1)} %scatter_custom_fusion.1) | copy-start | bytes 2359300
  401.4 27.5 %copy-start.1 = (bf16[4,4,384,256]{3,2,1,0:T(8,128)(2,1)S(1)}, bf16[4,4,384,256]{3,2,1,0:T(8,128)(2,1)}, u32[]{:S(2)}) copy-start(bf16[4,4,384,256]{3,2,1,0:T(8,128)(2,1)} %param.10) | copy-start | bytes 9437188
Sparse Core Ops, SparseCore 0:
  8.9 169.4 all-gather.3
  180.0 164.9 all-gather.5
